TPU v7x, 32 devices: a whole 2x2x4 slice. The times are simulated.
32 devices in a mesh: seq: 2 (over y), row: 4 (over x, core), col: 4 (over z).
Axes of the slice: x: 2, y: 2, z: 4, core: 2. Of those that a mesh axis runs over, the one named last changes fastest.
Arguments:
- tokens: bfloat16 [4096, 5376], P(('seq', 'row'), 'col'), may hold values from -6 to 6
- w_query: bfloat16 [5376, 4096], P(('seq', 'row'), 'col'), may hold values from -0.078125 to 0.078125
- key_weight: bfloat16 [5376, 2048], P(('seq', 'row'), 'col'), may hold values from -0.078125 to 0.078125
- value_weight: bfloat16 [5376, 2048], P(('seq', 'row'), 'col'), may hold values from -0.078125 to 0.078125
- w_output: bfloat16 [4096, 5376], P(('seq', 'row'), 'col'), may hold values from -0.09375 to 0.09375
- query_gain: float32 [128], replicated, may hold values from 0.5 to 8
- key_gain: float32 [128], replicated, may hold values from 0.5 to 8
Outputs:
- attended: bfloat16 [4096, 5376], P(('seq', 'row'), 'col')
All inputs are finite; a program needn't handle non-finite values.
Results may differ from a plain program's by a relative error of at most 0.0085.
The roundings to bfloat16 on the way count: a program that leaves them out, or rounds other values in their place, can miss the bound.
Values may be sent and summed in bfloat16 or wider, within the bound.
A program may use at most 128 MiB of HBM per device.

v0:
```python
import jax
import jax.numpy as jnp
from jax import lax
from jax.sharding import PartitionSpec as P

HEAD_SIZE = 128
WINDOW_KEYS = 1024
query_scale = 168.0 ** (-0.5)


def shifted(block, axis, distance):
    devices = range(lax.axis_size(axis))
    route = [(i - distance, i) for i in devices if i - distance in devices]
    return lax.ppermute(block, axis, route)


def head_norm(block, gain):
    mean_square = jnp.mean(block * block, axis=-1, keepdims=True)
    return block * lax.rsqrt(mean_square + 1e-06) * gain


def rotate(block, positions):
    half = block.shape[-1] // 2
    freqs = 10000.0 ** (-(jnp.arange(half, dtype=jnp.float32) * 2.0 / block.shape[-1]))
    angles = positions.astype(jnp.float32)[:, None] * freqs[None, :]
    cosine = jnp.cos(angles)[:, None, :]
    sine = jnp.sin(angles)[:, None, :]
    first = block[..., :half]
    second = block[..., half:]
    return jnp.concatenate(
        [first * cosine - second * sine, second * cosine + first * sine], axis=-1
    )


def attend(queries, key_states, value_states, qpos, kpos):
    rows = queries.shape[0]
    kv_heads = key_states.shape[1]
    grouped = queries.reshape(rows, kv_heads, 2, HEAD_SIZE)
    scores = (
        jnp.einsum("bhgd,khd->hgbk", grouped, key_states, preferred_element_type=jnp.float32)
        * query_scale
    )
    gap = qpos[:, None] - kpos[None, :]
    valid = (kpos[None, :] >= 0) & (gap >= 0) & (gap < WINDOW_KEYS)
    scores = jnp.where(valid[None, None], scores, -1e30)
    top = jnp.max(scores, axis=-1, keepdims=True)
    weights = jnp.exp(scores - top)
    weights = (weights / jnp.sum(weights, axis=-1, keepdims=True)).astype(jnp.bfloat16)
    mixed = jnp.einsum("hgbk,khd->bhgd", weights, value_states, preferred_element_type=jnp.float32)
    return mixed.astype(jnp.bfloat16).reshape(rows, kv_heads * 2 * HEAD_SIZE)


def shards(tokens, w_query, key_weight, value_weight, w_output, query_gain, key_gain):
    rows = tokens.shape[0]
    whole = lax.all_gather(tokens, "col", axis=1, tiled=True)
    columns = whole
    proj_q = jnp.dot(
        columns,
        lax.all_gather(w_query, ("seq", "row"), axis=0, tiled=True),
        preferred_element_type=jnp.float32,
    )
    projected_key = jnp.dot(
        columns,
        lax.all_gather(key_weight, ("seq", "row"), axis=0, tiled=True),
        preferred_element_type=jnp.float32,
    )
    proj_v = jnp.dot(
        columns,
        lax.all_gather(value_weight, ("seq", "row"), axis=0, tiled=True),
        preferred_element_type=jnp.float32,
    )
    base = lax.axis_index(("seq", "row")) * rows
    positions = base + jnp.arange(rows, dtype=jnp.int32)
    q_heads = proj_q.shape[1] // HEAD_SIZE
    kv_heads = projected_key.shape[1] // HEAD_SIZE
    queries = rotate(
        head_norm(proj_q.reshape(rows, q_heads, HEAD_SIZE), query_gain), positions
    ).astype(jnp.bfloat16)
    key_states = rotate(
        head_norm(projected_key.reshape(rows, kv_heads, HEAD_SIZE), key_gain), positions
    ).astype(jnp.bfloat16)
    key_flat = key_states.reshape(rows, kv_heads * HEAD_SIZE)
    value_flat = proj_v.astype(jnp.bfloat16)
    prior_one = shifted((key_flat, value_flat), ("seq", "row"), 1)
    prior_two = shifted((key_flat, value_flat), ("seq", "row"), 2)
    key_rows = jnp.concatenate([prior_two[0], prior_one[0], key_flat], axis=0).reshape(
        3 * rows, kv_heads, HEAD_SIZE
    )
    value_rows = jnp.concatenate([prior_two[1], prior_one[1], value_flat], axis=0).reshape(
        3 * rows, kv_heads, HEAD_SIZE
    )
    kpos = base - 2 * rows + jnp.arange(3 * rows, dtype=jnp.int32)
    mixed = attend(queries, key_rows, value_rows, positions, kpos)
    all_heads = lax.all_gather(mixed, "col", axis=1, tiled=True)
    columns = all_heads
    attended = jnp.dot(
        columns,
        lax.all_gather(w_output, ("seq", "row"), axis=0, tiled=True),
        preferred_element_type=jnp.float32,
    )
    return attended.astype(jnp.bfloat16)


def solution(mesh):
    return jax.shard_map(
        shards,
        mesh=mesh,
        in_specs=(
            P(("seq", "row"), "col"),
            P(("seq", "row"), "col"),
            P(("seq", "row"), "col"),
            P(("seq", "row"), "col"),
            P(("seq", "row"), "col"),
            P(),
            P(),
        ),
        out_specs=P(("seq", "row"), "col"),
        check_vma=False,
    )
```

profile of v0, /device:TPU:0, one launch (start us, length us, event | category | flops | bytes accessed | tf_op | source)
XLA Modules:
  0.0 458.2 jit_solution(17075732382961147357)
XLA Ops:
  6.5 0.0 all-gather.7.cloned.1.call-start
  6.5 0.7 all-gather.7.cloned.1.call-update
  7.3 0.0 all-gather.11.cloned.1.call-start
  7.3 0.7 all-gather.11.cloned.1.call-update
  8.0 0.0 all-gather.9.cloned.1.call-start
  8.1 0.7 all-gather.9.cloned.1.call-update
  8.7 0.0 all-gather.13.cloned.1.call-start
  8.8 0.5 all-gather.13.cloned.1.call-update
  9.3 0.0 all-gather.17.cloned.1.call-start
  9.4 0.5 all-gather.17.cloned.1.call-update
  9.9 0.0 all-gather.15.cloned.1.call-start
  10.0 1.0 multiply_cosine_fusion
  11.0 0.0 copy-start.2
  11.0 103.0 %all-gather.7.cloned.1.call-done = bf16[512,5376]{0,1:T(8,128)(2,1)} async-done(((bf16[512,1344]{0,1:T(8,128)(2,1)}), bf16[512,5376]{0,1:T(8,128)(2,1)}) %all-gather.7.cloned.1.call-update) | async-done | bytes 5505040 | tf_op jit(solution)/shard_map/all_gather | solution.py:55
  114.0 42.5 %all-gather.11.cloned.1.call-done = bf16[5376,512]{1,0:T(8,128)(2,1)} async-done(((bf16[672,512]{1,0:T(8,128)(2,1)}), bf16[5376,512]{1,0:T(8,128)(2,1)}) %all-gather.11.cloned.1.call-update) | async-done | bytes 5505040 | tf_op jit(solution)/shard_map/all_gather | solution.py:64
  156.5 6.7 %multiply_reduce_fusion.1 = (f32[512,4]{0,1:T(4,128)S(1)}, f32[512,512]{0,1:T(8,128)S(1)}) fusion(bf16[512,5376]{0,1:T(8,128)(2,1)} %all-gather.7.cloned.1.call-done, bf16[5376,512]{1,0:T(8,128)(2,1)} %all-gather.11.cloned.1.call-done), kind=kOutput, calls=%fused_computation.29 | convolution fusion | flops 2819094528 | bytes 12066816 | tf_op jit(solution)/shard_map/dot_general | solution.py:62
  163.2 0.3 copy.30
  163.6 0.0 copy-done.2
  163.6 0.3 multiply_multiply_fusion.1
  163.9 0.4 multiply_subtract_fusion
  164.4 0.3 maximum_convert_fusion
  164.7 0.2 copy.31
  164.9 3.4 collective-permute-start.2
  168.3 1.9 collective-permute-start.3
  170.3 39.0 %all-gather.9.cloned.1.call-done = bf16[5376,512]{1,0:T(8,128)(2,1)} async-done(((bf16[672,512]{1,0:T(8,128)(2,1)}), bf16[5376,512]{1,0:T(8,128)(2,1)}) %all-gather.9.cloned.1.call-update) | async-done | bytes 5505040 | tf_op jit(solution)/shard_map/all_gather | solution.py:69
  209.3 7.2 %convolution_convert_fusion.1 = bf16[512,512]{1,0:T(8,128)(2,1)S(1)} fusion(bf16[512,5376]{0,1:T(8,128)(2,1)} %all-gather.7.cloned.1.call-done, bf16[5376,512]{1,0:T(8,128)(2,1)} %all-gather.9.cloned.1.call-done), kind=kOutput, calls=%fused_computation.23 | convolution fusion | flops 2818834432 | bytes 11534336 | tf_op jit(solution)/shard_map/dot_general | solution.py:67
  216.5 3.1 collective-permute-start
  219.6 2.7 collective-permute-start.1
  222.2 2.0 fusion.9
  224.2 0.0 collective-permute-done.2
  224.2 1.0 copy.32
  225.2 0.0 collective-permute-done.3
  225.2 1.0 copy.33
  226.2 15.8 %collective-permute-done = bf16[512,512]{1,0:T(8,128)(2,1)} collective-permute-done((bf16[512,512]{1,0:T(8,128)(2,1)S(1)}, bf16[512,512]{1,0:T(8,128)(2,1)}, u32[]{:S(2)}, u32[]{:S(2)}) %collective-permute-start) | collective-permute-done | bytes 524320 | tf_op jit(solution)/shard_map/ppermute | solution.py:14
  242.0 0.0 collective-permute-done.1
  242.0 1.3 pad_maximum_fusion
  243.3 1.6 copy.43
  244.9 44.2 %all-gather.13.cloned.1.call-done = bf16[5376,1024]{1,0:T(8,128)(2,1)} async-done(((bf16[672,1024]{1,0:T(8,128)(2,1)}), bf16[5376,1024]{1,0:T(8,128)(2,1)}) %all-gather.13.cloned.1.call-update) | async-done | bytes 11010064 | tf_op jit(solution)/shard_map/all_gather | solution.py:59
  289.1 10.3 %convolution_bitcast_fusion = f32[64,8,8,128]{3,1,2,0:T(8,128)S(1)} fusion(bf16[512,5376]{0,1:T(8,128)(2,1)} %all-gather.7.cloned.1.call-done, bf16[5376,1024]{1,0:T(8,128)(2,1)} %all-gather.13.cloned.1.call-done), kind=kOutput, calls=%fused_computation.19 | convolution fusion | flops 5637144576 | bytes 18612224 | tf_op jit(solution)/shard_map/dot_general | solution.py:57
  299.4 0.0 copy-start.3
  299.4 0.5 copy.44
  299.9 0.6 multiply_reduce_fusion
  300.5 0.1 copy.34
  300.6 0.1 copy.35
  300.8 0.0 copy-done.3
  300.8 0.9 multiply_multiply_fusion
  301.6 0.9 subtract_convert_fusion
  302.5 0.0 copy-start
  302.5 0.0 copy-start.1
  302.5 0.1 copy.37
  302.7 0.1 copy.36
  302.8 0.7 copy-done
  303.6 0.2 copy-done.1
  303.7 11.8 %fusion.11 = f32[4,1536,512,2]{2,1,3,0:T(8,128)} fusion(bf16[512,4,128]{2,0,1:T(8,128)(2,1)S(1)} %maximum_convert_fusion, bf16[512,4,128]{2,0,1:T(8,128)(2,1)S(1)} %copy-done.1, bf16[512,4,128]{2,0,1:T(8,128)(2,1)S(1)} %copy-done, bf16[512,4,2,64]{3,0,2,1:T(8,128)(2,1)S(1)} %bitcast.51, bf16[512,4,2,64]{3,0,2,1:T(8,128)(2,1)S(1)} %bitcast.53), kind=kOutput, calls=%fused_computation.30 | convolution fusion | flops 1617428480 | bytes 27787264 | tf_op jit(solution)/shard_map/bhgd,khd->hgbk/dot_general | solution.py:40
  315.6 10.5 %fusion.23 = f32[4,2,512]{2,1,0:T(2,128)S(1)} fusion(pred[512,1536]{0,1:T(8,128)(4,1)} %fusion.9, bf16[512,4,128]{2,0,1:T(8,128)(2,1)S(1)} %maximum_convert_fusion, bf16[512,4,128]{2,0,1:T(8,128)(2,1)} %copy.33, bf16[512,4,128]{2,0,1:T(8,128)(2,1)S(1)} %copy-done, bf16[512,4,2,64]{3,0,2,1:T(8,128)(2,1)S(1)} %bitcast.52, bf16[512,4,2,64]{3,0,2,1:T(8,128)(2,1)S(1)} %bitcast.54), kind=kOutput, calls=%fused_computation.47 | convolution fusion | flops 1642595840 | bytes 3424256 | tf_op jit(solution)/shard_map/sub | solution.py:47
  326.1 15.4 %fusion.10 = bf16[4,128,2,512]{3,1,2,0:T(8,128)(2,1)} fusion(bf16[1536,4,128,1]{0,2,3,1:T(8,128)(2,1)} %bitcast.55, f32[4,2,512]{2,1,0:T(2,128)S(1)} %fusion.23, f32[4,1536,512,2]{2,1,3,0:T(8,128)} %fusion.11, pred[512,1536]{0,1:T(8,128)(4,1)} %fusion.9), kind=kOutput, calls=%fused_computation.22 | convolution fusion | flops 1642599936 | bytes 28590080 | tf_op jit(solution)/shard_map/hgbk,khd->bhgd/dot_general | solution.py:49
  341.4 0.0 all-gather.15.cloned.1.call-update
  341.5 17.0 %all-gather.17.cloned.1.call-done = bf16[4096,1344]{0,1:T(8,128)(2,1)} async-done(((bf16[512,1344]{0,1:T(8,128)(2,1)}), bf16[4096,1344]{0,1:T(8,128)(2,1)}) %all-gather.17.cloned.1.call-update) | async-done | bytes 11010064 | tf_op jit(solution)/shard_map/all_gather | solution.py:98
  358.5 82.2 %all-gather.15.cloned.1.call-done = bf16[512,4096]{0,1:T(8,128)(2,1)} async-done(((bf16[512,1024]{0,1:T(8,128)(2,1)}), bf16[512,4096]{0,1:T(8,128)(2,1)}) %all-gather.15.cloned.1.call-update) | async-done | bytes 4194320 | tf_op jit(solution)/shard_map/all_gather | solution.py:94
  440.7 10.7 %convolution_convert_fusion = bf16[512,1344]{0,1:T(8,128)(2,1)} fusion(bf16[4096,1344]{0,1:T(8,128)(2,1)} %all-gather.17.cloned.1.call-done, bf16[512,4096]{0,1:T(8,128)(2,1)} %all-gather.15.cloned.1.call-done), kind=kOutput, calls=%fused_computation.14 | convolution fusion | flops 5637832704 | bytes 16580608 | tf_op jit(solution)/shard_map/dot_general | solution.py:96
  (7 shorter events, 0.1 us)
Async XLA Ops:
  6.5 107.5 %all-gather.7.cloned.1.call-start = ((), (), s32[]{:S(2)}) async-start(), calls=%async_computation | async-start | bytes 6881280 | tf_op jit(solution)/shard_map/all_gather | solution.py:55
  7.3 149.3 %all-gather.11.cloned.1.call-start = ((), (), s32[]{:S(2)}) async-start(), calls=%async_computation.2 | async-start | bytes 6193152 | tf_op jit(solution)/shard_map/all_gather | solution.py:64
  8.0 201.3 %all-gather.9.cloned.1.call-start = ((), (), s32[]{:S(2)}) async-start(), calls=%async_computation.1 | async-start | bytes 6193152 | tf_op jit(solution)/shard_map/all_gather | solution.py:69
  8.7 280.4 %all-gather.13.cloned.1.call-start = ((), (), s32[]{:S(2)}) async-start(), calls=%async_computation.3 | async-start | bytes 12386304 | tf_op jit(solution)/shard_map/all_gather | solution.py:59
  9.3 349.2 %all-gather.17.cloned.1.call-start = ((), (), s32[]{:S(2)}) async-start(), calls=%async_computation.5 | async-start | bytes 12386304 | tf_op jit(solution)/shard_map/all_gather | solution.py:98
  9.9 430.8 %all-gather.15.cloned.1.call-start = ((), (), s32[]{:S(2)}) async-start(), calls=%async_computation.4 | async-start | bytes 5242880 | tf_op jit(solution)/shard_map/all_gather | solution.py:94
  11.0 152.6 %copy-start.2 = (f32[128]{0:T(128)S(1)}, f32[128]{0:T(128)}, u32[]{:S(2)}) copy-start(f32[128]{0:T(128)} %param.13) | copy-start | bytes 1540
  164.9 59.3 %collective-permute-start.2 = (bf16[512,512]{0,1:T(8,128)(2,1)S(1)}, bf16[512,512]{0,1:T(8,128)(2,1)S(1)}, u32[]{:S(2)}, u32[]{:S(2)}) collective-permute-start(bf16[512,512]{0,1:T(8,128)(2,1)S(1)} %bitcast.58), channel_id=1, source_target_pairs={{0,8},{4,12},{8,16},{12,20},{16,24},{20,28},{1,9},{5,13},{9,17},{1... | collective-permute-start | bytes 1572872 | tf_op jit(solution)/shard_map/ppermute | solution.py:14
  168.3 56.9 %collective-permute-start.3 = (bf16[512,512]{0,1:T(8,128)(2,1)S(1)}, bf16[512,512]{0,1:T(8,128)(2,1)S(1)}, u32[]{:S(2)}, u32[]{:S(2)}) collective-permute-start(bf16[512,512]{0,1:T(8,128)(2,1)S(1)} %bitcast.59), channel_id=1, source_target_pairs={{0,4},{4,8},{8,12},{12,16},{16,20},{20,24},{24,28},{1,5},{5,9},{9,... | collective-permute-start | bytes 1572872 | tf_op jit(solution)/shard_map/ppermute | solution.py:14
  216.5 25.5 %collective-permute-start = (bf16[512,512]{1,0:T(8,128)(2,1)S(1)}, bf16[512,512]{1,0:T(8,128)(2,1)}, u32[]{:S(2)}, u32[]{:S(2)}) collective-permute-start(bf16[512,512]{1,0:T(8,128)(2,1)S(1)} %convolution_convert_fusion.1), channel_id=1, source_target_pairs={{0,8},{4,12},{8,16},{12,20},{16,24},{20,28},{1,9},{5,13},{9,17},{1... | collective-permute-start | bytes 1572872 | tf_op jit(solution)/shard_map/ppermute | solution.py:14
  219.6 22.5 %collective-permute-start.1 = (bf16[512,512]{1,0:T(8,128)(2,1)S(1)}, bf16[512,512]{1,0:T(8,128)(2,1)}, u32[]{:S(2)}, u32[]{:S(2)}) collective-permute-start(bf16[512,512]{1,0:T(8,128)(2,1)S(1)} %convolution_convert_fusion.1), channel_id=1, source_target_pairs={{0,4},{4,8},{8,12},{12,16},{16,20},{20,24},{24,28},{1,5},{5,9},{9,... | collective-permute-start | bytes 1572872 | tf_op jit(solution)/shard_map/ppermute | solution.py:14
  299.4 1.4 copy-start.3
  302.5 1.1 copy-start
  302.5 1.2 copy-start.1
Sparse Core Ops, SparseCore 0:
  8.9 105.0 all-gather.6
  115.9 40.5 all-gather.10
  158.4 50.8 all-gather.8
  211.0 78.0 all-gather.12
  290.8 67.6 all-gather.16
  359.9 80.7 all-gather.14
where the time goes:
time: 458 us
  waiting for transfers between devices  347 us (76%)
  matrix products  72.6 us (16%)
  between operations  13.7 us (3%)
  starting transfers between devices  11.2 us (2%)
  other arithmetic  7.75 us (2%)
  local copies, waits for them, and re-layouts  6.03 us (1%)
    all_gather x1, waiting for transfers between devices, shards(): whole = lax.all_gather(tokens, 'col', axis=1, tiled=True)  103 us
    all_gather x1, waiting for transfers between devices, shards(): all_heads = lax.all_gather(mixed, 'col', axis=1, tiled=True)  82.2 us
    all_gather x1, waiting for transfers between devices, shards(): lax.all_gather(w_query, ('seq', 'row'), axis=0, tiled=True)  44.2 us
    all_gather x1, waiting for transfers between devices, shards(): lax.all_gather(key_weight, ('seq', 'row'), axis=0, tiled=True)  42.5 us
    all_gather x1, waiting for transfers between devices, shards(): lax.all_gather(value_weight, ('seq', 'row'), axis=0, tiled=True)  39 us
    all_gather x1, waiting for transfers between devices, shards(): lax.all_gather(w_output, ('seq', 'row'), axis=0, tiled=True)  17 us
    ppermute x4, waiting for transfers between devices, shifted(): return lax.ppermute(block, axis, route)  15.8 us
    dot_general x1, matrix products, attend(): jnp.einsum('hgbk,khd->bhgd', weights, value_states, preferred_element_typ...  15.4 us
  transfers between devices with their start and end apart: 10, of which 7 were waited for; matrix products, arithmetic and copies ran while one was open for 16% of the time, Pallas kernels for 0%

commit v1 on v0

--- a/solution.py
+++ b/solution.py
@@ -6,6 +6,17 @@
 HEAD_SIZE = 128
 WINDOW_KEYS = 1024
 query_scale = 168.0 ** (-0.5)
+
+
+def turned_line(value, axis, dim):
+    devices = lax.axis_size(axis)
+    route = [(i, (i + 1) % devices) for i in range(devices)]
+    shards = [value]
+    for stride in range(1, devices):
+        shards = [lax.ppermute(shards[0], axis, route), *shards]
+    full = jnp.concatenate(shards, axis=dim)
+    shift = (lax.axis_index(axis) + 1) * shards[-1].shape[dim]
+    return jnp.roll(full, shift, axis=dim)
 
 
 def shifted(block, axis, distance):
@@ -91,7 +102,7 @@
     )
     kpos = base - 2 * rows + jnp.arange(3 * rows, dtype=jnp.int32)
     mixed = attend(queries, key_rows, value_rows, positions, kpos)
-    all_heads = lax.all_gather(mixed, "col", axis=1, tiled=True)
+    all_heads = turned_line(mixed, "col", 1)
     columns = all_heads
     attended = jnp.dot(
         columns,

time: 458 us -> 448 us (0.978)
  waiting for transfers between devices: 347 us -> 325 us
  local copies, waits for them, and re-layouts: 6.03 us -> 16.2 us
    all_gather x1 -> x0, waiting for transfers between devices: 82.2 us -> none  [shards(): all_heads = lax.all_gather(mixed, 'col', axis=1, tiled=True)]
    ppermute x0 -> x3, waiting for transfers between devices: none -> 77.4 us  [turned_line(): shards = [lax.ppermute(shards[0], axis, route), *shards]]
    all_gather x1, waiting for transfers between devices: 17 us -> 0.01 us  [shards(): lax.all_gather(w_output, ('seq', 'row'), axis=0, tiled=True)]
    unnamed x9 -> x18, local copies, waits for them, and re-layouts: 1.4 us -> 10.4 us
  transfers between devices with their start and end apart: 10 -> 12, of which waited for: 7 -> 8; matrix products, arithmetic and copies ran while one was open for 16% -> 19% of each run, Pallas kernels for 0% -> 0%
where the time goes in v1:
time: 448 us; the launch traced here: 447 us
  waiting for transfers between devices  325 us (73%)
  matrix products  72.1 us (16%)
  local copies, waits for them, and re-layouts  16.2 us (4%)
  between operations  13.4 us (3%)
  starting transfers between devices  12.8 us (3%)
  other arithmetic  7.73 us (2%)
    all_gather x1, waiting for transfers between devices, shards(): whole = lax.all_gather(tokens, 'col', axis=1, tiled=True)  103 us
    ppermute x3, waiting for transfers between devices, turned_line(): shards = [lax.ppermute(shards[0], axis, route), *shards]  77.4 us
    all_gather x1, waiting for transfers between devices, shards(): lax.all_gather(w_query, ('seq', 'row'), axis=0, tiled=True)  44.2 us
    all_gather x1, waiting for transfers between devices, shards(): lax.all_gather(key_weight, ('seq', 'row'), axis=0, tiled=True)  42.5 us
    all_gather x1, waiting for transfers between devices, shards(): lax.all_gather(value_weight, ('seq', 'row'), axis=0, tiled=True)  39 us
    ppermute x4, waiting for transfers between devices, shifted(): return lax.ppermute(block, axis, route)  15.8 us
    dot_general x1, matrix products, attend(): jnp.einsum('hgbk,khd->bhgd', weights, value_states, preferred_element_typ...  14.7 us
    dot_general x1, matrix products, attend(): jnp.einsum('bhgd,khd->hgbk', grouped, key_states, preferred_element_type=...  11.8 us
  transfers between devices with their start and end apart: 12, of which 8 were waited for; matrix products, arithmetic and copies ran while one was open for 19% of the time, Pallas kernels for 0%

profile of v1, /device:TPU:0, one launch (start us, length us, event | category | flops | bytes accessed | tf_op | source)
XLA Modules:
  0.0 447.3 jit_solution(10434675050669129227)
XLA Ops:
  6.5 0.7 all-gather.6.cloned.1.call-update
  7.3 0.0 all-gather.10.cloned.1.call-start
  7.3 0.7 all-gather.10.cloned.1.call-update
  8.0 0.0 all-gather.8.cloned.1.call-start
  8.1 0.7 all-gather.8.cloned.1.call-update
  8.7 0.0 all-gather.12.cloned.1.call-start
  8.8 0.5 all-gather.12.cloned.1.call-update
  9.3 0.0 all-gather.14.cloned.1.call-start
  9.4 0.5 all-gather.14.cloned.1.call-update
  10.0 1.0 multiply_cosine_fusion
  11.0 0.0 copy-start.3
  11.0 103.1 %all-gather.6.cloned.1.call-done = bf16[512,5376]{0,1:T(8,128)(2,1)} async-done(((bf16[512,1344]{0,1:T(8,128)(2,1)}), bf16[512,5376]{0,1:T(8,128)(2,1)}) %all-gather.6.cloned.1.call-update) | async-done | bytes 5505040 | tf_op jit(solution)/shard_map/all_gather | solution.py:66
  114.0 42.5 %all-gather.10.cloned.1.call-done = bf16[5376,512]{1,0:T(8,128)(2,1)} async-done(((bf16[672,512]{1,0:T(8,128)(2,1)}), bf16[5376,512]{1,0:T(8,128)(2,1)}) %all-gather.10.cloned.1.call-update) | async-done | bytes 5505040 | tf_op jit(solution)/shard_map/all_gather | solution.py:75
  156.5 6.7 %multiply_reduce_fusion.1 = (f32[512,4]{0,1:T(4,128)S(1)}, f32[512,512]{0,1:T(8,128)S(1)}) fusion(bf16[512,5376]{0,1:T(8,128)(2,1)} %all-gather.6.cloned.1.call-done, bf16[5376,512]{1,0:T(8,128)(2,1)} %all-gather.10.cloned.1.call-done), kind=kOutput, calls=%fused_computation.31 | convolution fusion | flops 2819094528 | bytes 12066816 | tf_op jit(solution)/shard_map/dot_general | solution.py:73
  163.2 0.3 copy.30
  163.6 0.3 multiply_multiply_fusion.1
  163.9 0.4 multiply_subtract_fusion
  164.4 0.3 maximum_convert_fusion
  164.7 0.2 copy.31
  164.9 3.4 collective-permute-start.2
  168.3 1.9 collective-permute-start.3
  170.3 39.0 %all-gather.8.cloned.1.call-done = bf16[5376,512]{1,0:T(8,128)(2,1)} async-done(((bf16[672,512]{1,0:T(8,128)(2,1)}), bf16[5376,512]{1,0:T(8,128)(2,1)}) %all-gather.8.cloned.1.call-update) | async-done | bytes 5505040 | tf_op jit(solution)/shard_map/all_gather | solution.py:80
  209.3 7.2 %convolution_convert_fusion = bf16[512,512]{1,0:T(8,128)(2,1)S(1)} fusion(bf16[512,5376]{0,1:T(8,128)(2,1)} %all-gather.6.cloned.1.call-done, bf16[5376,512]{1,0:T(8,128)(2,1)} %all-gather.8.cloned.1.call-done), kind=kOutput, calls=%fused_computation.25 | convolution fusion | flops 2818834432 | bytes 11534336 | tf_op jit(solution)/shard_map/dot_general | solution.py:78
  216.5 3.1 collective-permute-start
  219.6 2.7 collective-permute-start.1
  222.2 2.0 fusion.11
  224.2 0.0 collective-permute-done.2
  224.2 1.0 copy.32
  225.2 0.0 collective-permute-done.3
  225.2 1.0 copy.33
  226.3 15.8 %collective-permute-done = bf16[512,512]{1,0:T(8,128)(2,1)} collective-permute-done((bf16[512,512]{1,0:T(8,128)(2,1)S(1)}, bf16[512,512]{1,0:T(8,128)(2,1)}, u32[]{:S(2)}, u32[]{:S(2)}) %collective-permute-start) | collective-permute-done | bytes 524320 | tf_op jit(solution)/shard_map/ppermute | solution.py:25
  242.0 0.0 collective-permute-done.1
  242.0 1.3 pad_maximum_fusion
  243.3 1.6 copy.43
  244.9 44.2 %all-gather.12.cloned.1.call-done = bf16[5376,1024]{1,0:T(8,128)(2,1)} async-done(((bf16[672,1024]{1,0:T(8,128)(2,1)}), bf16[5376,1024]{1,0:T(8,128)(2,1)}) %all-gather.12.cloned.1.call-update) | async-done | bytes 11010064 | tf_op jit(solution)/shard_map/all_gather | solution.py:70
  289.1 10.3 %convolution_bitcast_fusion = f32[64,8,8,128]{3,1,2,0:T(8,128)S(1)} fusion(bf16[512,5376]{0,1:T(8,128)(2,1)} %all-gather.6.cloned.1.call-done, bf16[5376,1024]{1,0:T(8,128)(2,1)} %all-gather.12.cloned.1.call-done), kind=kOutput, calls=%fused_computation.21 | convolution fusion | flops 5637144576 | bytes 18612224 | tf_op jit(solution)/shard_map/dot_general | solution.py:68
  299.4 0.0 copy-start.4
  299.4 0.5 copy.44
  299.9 0.6 multiply_reduce_fusion
  300.5 0.1 copy.34
  300.6 0.1 copy.35
  300.8 0.9 multiply_multiply_fusion
  301.6 0.9 subtract_convert_fusion
  302.5 0.1 copy.37
  302.7 0.1 copy.36
  302.8 0.1 copy-done.2
  302.9 11.8 %fusion.16 = f32[4,1536,512,2]{2,1,3,0:T(8,128)} fusion(bf16[512,4,128]{2,0,1:T(8,128)(2,1)S(1)} %maximum_convert_fusion, bf16[512,4,128]{2,0,1:T(8,128)(2,1)S(1)} %copy-done.2, bf16[512,4,128]{2,0,1:T(8,128)(2,1)S(1)} %copy-done, bf16[512,4,2,64]{3,0,2,1:T(8,128)(2,1)S(1)} %bitcast.50, bf16[512,4,2,64]{3,0,2,1:T(8,128)(2,1)S(1)} %bitcast.52), kind=kOutput, calls=%fused_computation.32 | convolution fusion | flops 1617428480 | bytes 27787264 | tf_op jit(solution)/shard_map/bhgd,khd->hgbk/dot_general | solution.py:51
  314.7 10.8 %fusion.29 = f32[4,2,512]{2,1,0:T(2,128)S(1)} fusion(pred[512,1536]{0,1:T(8,128)(4,1)} %fusion.11, bf16[512,4,128]{2,0,1:T(8,128)(2,1)S(1)} %maximum_convert_fusion, bf16[512,4,128]{2,0,1:T(8,128)(2,1)} %copy.33, bf16[512,4,128]{2,0,1:T(8,128)(2,1)S(1)} %copy-done.1, bf16[512,4,2,64]{3,0,2,1:T(8,128)(2,1)S(1)} %bitcast.51, ...), kind=kOutput, calls=%fused_computation.58 | convolution fusion | flops 1642595840 | bytes 3424256 | tf_op jit(solution)/shard_map/sub | solution.py:58
  325.5 14.7 %fusion.15 = bf16[4,128,2,512]{3,1,2,0:T(8,128)(2,1)S(1)} fusion(bf16[1536,4,128,1]{0,2,3,1:T(8,128)(2,1)} %bitcast.57, f32[4,2,512]{2,1,0:T(2,128)S(1)} %fusion.29, f32[4,1536,512,2]{2,1,3,0:T(8,128)} %fusion.16, pred[512,1536]{0,1:T(8,128)(4,1)} %fusion.11), kind=kOutput, calls=%fused_computation.24 | convolution fusion | flops 1642599936 | bytes 28590080 | tf_op jit(solution)/shard_map/hgbk,khd->bhgd/dot_general | solution.py:60
  340.1 1.6 collective-permute-start.4
  341.7 25.6 %collective-permute-done.4 = bf16[512,1024]{0,1:T(8,128)(2,1)S(1)} collective-permute-done((bf16[512,1024]{0,1:T(8,128)(2,1)S(1)}, bf16[512,1024]{0,1:T(8,128)(2,1)S(1)}, u32[]{:S(2)}, u32[]{:S(2)}) %collective-permute-start.4) | collective-permute-done | bytes 1048608 | tf_op jit(solution)/shard_map/ppermute | solution.py:16
  367.3 0.0 collective-permute-start.5
  367.3 26.3 %collective-permute-done.5 = bf16[512,1024]{0,1:T(8,128)(2,1)S(1)} collective-permute-done((bf16[512,1024]{0,1:T(8,128)(2,1)S(1)}, bf16[512,1024]{0,1:T(8,128)(2,1)S(1)}, u32[]{:S(2)}, u32[]{:S(2)}) %collective-permute-start.5) | collective-permute-done | bytes 1048608 | tf_op jit(solution)/shard_map/ppermute | solution.py:16
  393.6 0.0 collective-permute-start.6
  393.6 25.5 %collective-permute-done.6 = bf16[512,1024]{0,1:T(8,128)(2,1)} collective-permute-done((bf16[512,1024]{0,1:T(8,128)(2,1)S(1)}, bf16[512,1024]{0,1:T(8,128)(2,1)}, u32[]{:S(2)}, u32[]{:S(2)}) %collective-permute-start.6) | collective-permute-done | bytes 1048608 | tf_op jit(solution)/shard_map/ppermute | solution.py:16
  419.1 2.3 constant_dynamic-update-slice_fusion.7
  421.4 1.1 constant_dynamic-update-slice_fusion.6
  422.4 1.0 constant_dynamic-update-slice_fusion.5
  423.5 1.1 constant_dynamic-update-slice_fusion.4
  424.6 2.3 constant_dynamic-update-slice_fusion.3
  426.8 1.1 constant_dynamic-update-slice_fusion.2
  427.9 1.1 constant_dynamic-update-slice_fusion.1
  429.0 1.1 constant_dynamic-update-slice_fusion
  430.1 10.7 %fusion.12 = bf16[512,1344]{0,1:T(8,128)(2,1)} fusion(bf16[4096,1344]{0,1:T(8,128)(2,1)} %all-gather.14.cloned.1.call-done, bf16[512,8192]{0,1:T(8,128)(2,1)} %constant_dynamic-update-slice_fusion, s32[]{:T(128)S(6)} %select_n.19), kind=kOutput, calls=%fused_computation.16 | convolution fusion | flops 5637832704 | bytes 16580612 | tf_op jit(solution)/shard_map/dot_general | solution.py:107
  (16 shorter events, 0.1 us)
Async XLA Ops:
  6.5 107.5 %all-gather.6.cloned.1.call-start = ((), (), s32[]{:S(2)}) async-start(), calls=%async_computation | async-start | bytes 6881280 | tf_op jit(solution)/shard_map/all_gather | solution.py:66
  7.3 149.3 %all-gather.10.cloned.1.call-start = ((), (), s32[]{:S(2)}) async-start(), calls=%async_computation.2 | async-start | bytes 6193152 | tf_op jit(solution)/shard_map/all_gather | solution.py:75
  8.0 201.3 %all-gather.8.cloned.1.call-start = ((), (), s32[]{:S(2)}) async-start(), calls=%async_computation.1 | async-start | bytes 6193152 | tf_op jit(solution)/shard_map/all_gather | solution.py:80
  8.7 280.4 %all-gather.12.cloned.1.call-start = ((), (), s32[]{:S(2)}) async-start(), calls=%async_computation.3 | async-start | bytes 12386304 | tf_op jit(solution)/shard_map/all_gather | solution.py:70
  9.3 420.8 %all-gather.14.cloned.1.call-start = ((), (), s32[]{:S(2)}) async-start(), calls=%async_computation.4 | async-start | bytes 12386304 | tf_op jit(solution)/shard_map/all_gather | solution.py:109
  11.0 152.6 %copy-start.3 = (f32[128]{0:T(128)S(1)}, f32[128]{0:T(128)}, u32[]{:S(2)}) copy-start(f32[128]{0:T(128)} %param.13) | copy-start | bytes 1540
  164.9 59.3 %collective-permute-start.2 = (bf16[512,512]{0,1:T(8,128)(2,1)S(1)}, bf16[512,512]{0,1:T(8,128)(2,1)S(1)}, u32[]{:S(2)}, u32[]{:S(2)}) collective-permute-start(bf16[512,512]{0,1:T(8,128)(2,1)S(1)} %bitcast.59), channel_id=1, source_target_pairs={{0,8},{4,12},{8,16},{12,20},{16,24},{20,28},{1,9},{5,13},{9,17},{1... | collective-permute-start | bytes 1572872 | tf_op jit(solution)/shard_map/ppermute | solution.py:25
  168.3 56.9 %collective-permute-start.3 = (bf16[512,512]{0,1:T(8,128)(2,1)S(1)}, bf16[512,512]{0,1:T(8,128)(2,1)S(1)}, u32[]{:S(2)}, u32[]{:S(2)}) collective-permute-start(bf16[512,512]{0,1:T(8,128)(2,1)S(1)} %bitcast.60), channel_id=1, source_target_pairs={{0,4},{4,8},{8,12},{12,16},{16,20},{20,24},{24,28},{1,5},{5,9},{9,... | collective-permute-start | bytes 1572872 | tf_op jit(solution)/shard_map/ppermute | solution.py:25
  216.5 25.5 %collective-permute-start = (bf16[512,512]{1,0:T(8,128)(2,1)S(1)}, bf16[512,512]{1,0:T(8,128)(2,1)}, u32[]{:S(2)}, u32[]{:S(2)}) collective-permute-start(bf16[512,512]{1,0:T(8,128)(2,1)S(1)} %convolution_convert_fusion), channel_id=1, source_target_pairs={{0,8},{4,12},{8,16},{12,20},{16,24},{20,28},{1,9},{5,13},{9,17},{1... | collective-permute-start | bytes 1572872 | tf_op jit(solution)/shard_map/ppermute | solution.py:25
  219.6 22.5 %collective-permute-start.1 = (bf16[512,512]{1,0:T(8,128)(2,1)S(1)}, bf16[512,512]{1,0:T(8,128)(2,1)}, u32[]{:S(2)}, u32[]{:S(2)}) collective-permute-start(bf16[512,512]{1,0:T(8,128)(2,1)S(1)} %convolution_convert_fusion), channel_id=1, source_target_pairs={{0,4},{4,8},{8,12},{12,16},{16,20},{20,24},{24,28},{1,5},{5,9},{9,... | collective-permute-start | bytes 1572872 | tf_op jit(solution)/shard_map/ppermute | solution.py:25
  299.4 1.4 copy-start.4
  301.6 1.2 copy-start
  301.6 1.2 copy-start.2
  302.9 11.8 %copy-start.1 = (bf16[512,4,128]{2,0,1:T(8,128)(2,1)S(1)}, bf16[512,4,128]{2,0,1:T(8,128)(2,1)}, u32[]{:S(2)}) copy-start(bf16[512,4,128]{2,0,1:T(8,128)(2,1)} %copy.32) | copy-start | bytes 1572868
  340.1 27.2 %collective-permute-start.4 = (bf16[512,1024]{0,1:T(8,128)(2,1)S(1)}, bf16[512,1024]{0,1:T(8,128)(2,1)S(1)}, u32[]{:S(2)}, u32[]{:S(2)}) collective-permute-start(bf16[512,1024]{0,1:T(8,128)(2,1)S(1)} %bitcast.54), channel_id=1, source_target_pairs={{0,1},{1,2},{2,3},{3,0},{4,5},{5,6},{6,7},{7,4},{8,9},{9,10},{10,1... | collective-permute-start | bytes 3145736 | tf_op jit(solution)/shard_map/ppermute | solution.py:16
  367.3 26.3 %collective-permute-start.5 = (bf16[512,1024]{0,1:T(8,128)(2,1)S(1)}, bf16[512,1024]{0,1:T(8,128)(2,1)S(1)}, u32[]{:S(2)}, u32[]{:S(2)}) collective-permute-start(bf16[512,1024]{0,1:T(8,128)(2,1)S(1)} %collective-permute-done.4), channel_id=1, source_target_pairs={{0,1},{1,2},{2,3},{3,0},{4,5},{5,6},{6,7},{7,4},{8,9},{9,10},{10,1... | collective-permute-start | bytes 3145736 | tf_op jit(solution)/shard_map/ppermute | solution.py:16
  393.6 25.5 %collective-permute-start.6 = (bf16[512,1024]{0,1:T(8,128)(2,1)S(1)}, bf16[512,1024]{0,1:T(8,128)(2,1)}, u32[]{:S(2)}, u32[]{:S(2)}) collective-permute-start(bf16[512,1024]{0,1:T(8,128)(2,1)S(1)} %collective-permute-done.5), channel_id=1, source_target_pairs={{0,1},{1,2},{2,3},{3,0},{4,5},{5,6},{6,7},{7,4},{8,9},{9,10},{10,1... | collective-permute-start | bytes 3145736 | tf_op jit(solution)/shard_map/ppermute | solution.py:16
Sparse Core Ops, SparseCore 0:
  8.9 105.0 all-gather.5
  115.9 40.5 all-gather.9
  158.4 50.8 all-gather.7
  211.0 78.0 all-gather.11
  290.8 67.6 all-gather.13
